TPU v7x, 32 devices: a whole 2x2x4 slice. The times are simulated.
32 devices in a mesh: clip: 2 (over y), tm: 4 (over x, core), mp: 4 (over z).
Axes of the slice: x: 2, y: 2, z: 4, core: 2. Of those that a mesh axis runs over, the one named last changes fastest.
Arguments:
- token_ids: int32 [8, 256], P(('clip', 'tm')), parts along dimension 0, may hold values from 0 to 1023
- remask: int32 [8, 256], P(('clip', 'tm')), parts along dimension 0, may hold values from -1 to 255, as said below
- position_embed: bfloat16 [4, 256, 1024], P('tm'), may hold values from -0.625 to 0.625
- mask_embed: bfloat16 [1024], replicated, may hold values from -0.625 to 0.625
- table: bfloat16 [1024, 1024], P('mp')
- gain_in: float32 [1024], replicated, may hold values from 0.5 to 1.5
- gain_out: float32 [1024], replicated, may hold values from 0.5 to 1.5
- w_qkv: bfloat16 [3, 1024, 1024], P(None, None, 'mp')
- w_out: bfloat16 [1024, 1024], P('mp'), may hold values from -0.1875 to 0.1875
Outputs:
- log_probs: bfloat16 [8, 256, 1024], P(('clip', 'tm'), None, 'mp'), parts along dimension 0
- confidence: float32 [8, 256], P(('clip', 'tm')), parts along dimension 0
- clip_stats: float32 [4], P('clip'), parts along dimension 0
There are 2 independent parts, one for each index of `clip`. A program takes and returns all parts, laid end to end along the dimension named above; an argument that names none is the same for every part. Nothing has to cross between parts.
Inputs may be any that keep to these rules, and one draw needn't show every extreme that they name: `remask`: row f lists distinct masked positions of frame f in its first slots and -1 in the unused ones; every frame lists at least one position.
All inputs are finite; a program needn't handle non-finite values.
Results may differ from a plain program's by a relative error of at most 0.019.
The roundings to bfloat16 on the way count: a program that leaves them out, or rounds other values in their place, can miss the bound.
Values may be sent and summed in bfloat16 or wider, within the bound.
No kernel may reach another device: no remote copies, remote signals or barrier semaphores. Data moves between devices by JAX's collectives and lax.ppermute only.
A program may use at most 64 MiB of HBM per device.

v0:
```python
import math
import jax
import jax.numpy as jnp
from jax import lax
from jax.sharding import PartitionSpec as P

HEAD_DIM = 64


def layer_norm(values, gain):
    center = values - jnp.mean(values, axis=-1, keepdims=True)
    spread = jnp.mean(center * center, axis=-1, keepdims=True)
    return center * lax.rsqrt(spread + 1e-05) * gain


def absorb_block(state, query, key_block, value_block):
    running, totals, summed = state
    scores = jnp.einsum(
        "qhd,khd->hqk", query, key_block, preferred_element_type=jnp.float32
    ) * HEAD_DIM ** (-0.5)
    raised = jnp.maximum(running, jnp.max(scores, axis=-1))
    fade = jnp.exp(running - raised)
    weights = jnp.exp(scores - raised[:, :, None])
    totals = totals * fade + jnp.sum(weights, axis=-1)
    summed = summed * fade[:, :, None] + jnp.einsum(
        "hqk,khd->hqd",
        weights.astype(jnp.bfloat16),
        value_block,
        preferred_element_type=jnp.float32,
    )
    return (raised, totals, summed)


def sweep_keys(state, query, key_rows, value_rows):
    count = key_rows.shape[0]
    block = math.gcd(count, 512)
    heads_here = query.shape[1]
    key_blocks = key_rows.reshape(count // block, block, heads_here, HEAD_DIM)
    value_blocks = value_rows.reshape(count // block, block, heads_here, HEAD_DIM)

    def advance(inner, pair):
        return (absorb_block(inner, query, pair[0], pair[1]), None)

    state, ignored = lax.scan(advance, state, (key_blocks, value_blocks))
    return state


def empty_state(heads_here, row_count):
    return (
        jnp.full((heads_here, row_count), -1e30, jnp.float32),
        jnp.zeros((heads_here, row_count), jnp.float32),
        jnp.zeros((heads_here, row_count, HEAD_DIM), jnp.float32),
    )


def body(token_ids, remask, position_embed, mask_embed, table, gain_in, gain_out, w_qkv, w_out):
    frames_here, frame_span = token_ids.shape
    row_count = frames_here * frame_span
    parts_mp = lax.axis_size("mp")
    vocab_here = table.shape[0]
    local_width = w_qkv.shape[2]
    heads_here = local_width // HEAD_DIM
    offset = lax.axis_index("mp") * vocab_here
    spots = jnp.arange(frame_span, dtype=jnp.int32)
    masked = jnp.any(remask[:, None, :] == spots[None, :, None], axis=-1).reshape(row_count)
    flat_ids = token_ids.reshape(row_count)
    entries = offset + jnp.arange(vocab_here, dtype=jnp.int32)
    onehot = ((flat_ids[:, None] == entries[None, :]) & jnp.logical_not(masked)[:, None]).astype(
        jnp.bfloat16
    )
    added_rows = jnp.where(masked[:, None], mask_embed.astype(jnp.float32)[None, :], 0.0)
    added_rows = added_rows + position_embed.reshape(row_count, -1).astype(jnp.float32)
    share = row_count // parts_mp
    first_row = lax.axis_index("mp") * share
    looked = lax.psum_scatter(
        jnp.dot(onehot, table, preferred_element_type=jnp.float32).astype(jnp.bfloat16),
        "mp",
        scatter_dimension=0,
        tiled=True,
    ).astype(jnp.float32)
    hidden_in = looked + lax.dynamic_slice_in_dim(added_rows, first_row, share, 0)
    normed = layer_norm(hidden_in, gain_in).astype(jnp.bfloat16)
    projected = jnp.einsum(
        "rd,jdc->jrc",
        lax.all_gather(normed, "mp", axis=0, tiled=True),
        w_qkv,
        preferred_element_type=jnp.float32,
    ).astype(jnp.bfloat16)
    query = projected[0].reshape(row_count, heads_here, HEAD_DIM)
    keys = projected[1]
    values = projected[2]
    highest, totals, summed = sweep_keys(
        empty_state(heads_here, row_count),
        query,
        lax.all_gather(keys, "tm", axis=0, tiled=True),
        lax.all_gather(values, "tm", axis=0, tiled=True),
    )
    context = (
        (summed / totals[:, :, None])
        .transpose(1, 0, 2)
        .reshape(row_count, local_width)
        .astype(jnp.bfloat16)
    )
    mixed_rows = lax.psum_scatter(
        jnp.dot(context, w_out, preferred_element_type=jnp.float32),
        "mp",
        scatter_dimension=0,
        tiled=True,
    )
    final_local = layer_norm(hidden_in + mixed_rows, gain_out).astype(jnp.bfloat16)
    logits = lax.dot_general(
        lax.all_gather(final_local, "mp", axis=0, tiled=True),
        table,
        (((1,), (1,)), ((), ())),
        preferred_element_type=jnp.float32,
    )
    local_max = jnp.max(logits, axis=-1)
    row_max = lax.pmax(local_max, "mp")
    row_total = lax.psum(jnp.sum(jnp.exp(logits - row_max[:, None]), axis=-1), "mp")
    log_total = row_max + jnp.log(row_total)
    log_probs = (
        (logits - log_total[:, None])
        .astype(jnp.bfloat16)
        .reshape(frames_here, frame_span, vocab_here)
    )
    confidence = jnp.exp(row_max - log_total)
    weight = masked.astype(jnp.float32)
    conf_sum, count = lax.psum((jnp.sum(confidence * weight), jnp.sum(weight)), "tm")
    tokens_all = row_count * lax.axis_size("tm")
    clip_stats = jnp.stack([conf_sum / count, jnp.log(count / tokens_all)])
    return (log_probs, confidence.reshape(frames_here, frame_span), clip_stats)


def solution(mesh):
    return jax.shard_map(
        body,
        mesh=mesh,
        in_specs=(
            P(("clip", "tm"), None),
            P(("clip", "tm"), None),
            P("tm", None, None),
            P(),
            P("mp", None),
            P(),
            P(),
            P(None, None, "mp"),
            P("mp", None),
        ),
        out_specs=(P(("clip", "tm"), None, "mp"), P(("clip", "tm"), None), P("clip")),
        check_vma=False,
    )
```

profile of v0, /device:TPU:0, one launch (start us, length us, event | category | flops | bytes accessed | tf_op | source)
XLA Modules:
  0.0 160.6 jit_solution(13981228685784389720)
XLA Ops:
  7.2 0.0 copy-start
  7.2 0.0 copy-start.7
  7.2 0.0 reduce-scatter.3.cloned.1.call-start
  7.2 0.9 fusion.18
  8.1 0.0 copy-start.9
  8.2 2.2 %convolution_convert_fusion = bf16[256,1024]{1,0:T(8,128)(2,1)} fusion(bf16[256,1024]{1,0:T(8,128)(2,1)} %param.15, s32[256]{0:T(256)S(1)} %iota_add_fusion, s32[256]{0:T(256)} %bitcast.66, pred[256]{0:T(512)(128)(4,1)S(1)} %not.7), kind=kOutput, calls=%fused_computation.21 | convolution fusion | flops 134610944 | bytes 1050880 | tf_op jit(solution)/shard_map/dot_general | solution.py:76
  10.4 0.0 reduce-scatter.3.cloned.1.call-update
  10.4 0.0 reduce-scatter.5.cloned.1.call-start
  10.5 0.1 dynamic-slice
  10.6 0.0 copy-start.5
  10.6 0.7 convert_element_type.48
  11.3 23.9 %reduce-scatter.3.cloned.1.call-done = bf16[64,1024]{1,0:T(8,128)(2,1)} async-done(((bf16[256,1024]{1,0:T(8,128)(2,1)}), bf16[64,1024]{1,0:T(8,128)(2,1)}) %reduce-scatter.3.cloned.1.call-update) | async-done | bytes 131088 | tf_op jit(solution)/shard_map/reduce_scatter | solution.py:75
  35.1 0.0 copy-done.9
  35.1 1.2 fusion.26
  36.3 1.2 multiply_reduce_fusion.1
  37.6 0.0 copy-done.7
  37.6 1.1 multiply_convert_fusion.1
  38.7 15.5 %all_gather.12 = bf16[256,1024]{1,0:T(8,128)(2,1)S(1)} all-gather(bf16[64,1024]{1,0:T(8,128)(2,1)S(1)} %multiply_convert_fusion.1), channel_id=1, replica_groups=mesh['clip'=2,'tm'=4,'mp'=4] {'mp'}, dimensions={0}, use_global_device_ids=true | all-gather | bytes 655360 | tf_op jit(solution)/shard_map/all_gather | solution.py:85
  54.2 0.0 copy-done
  54.2 0.7 fusion.15
  54.9 0.0 copy-done.5
  55.0 7.1 %all-gather = bf16[1,1024,256]{1,2,0:T(8,128)(2,1)S(1)} all-gather(bf16[1,256,256]{1,2,0:T(8,128)(2,1)S(1)} %get-tuple-element.114), channel_id=2, replica_groups=mesh['clip'=2,'tm'=4,'mp'=4] {'tm'}, dimensions={1}, use_global_device_ids=true | all-gather | bytes 655360 | tf_op jit(solution)/shard_map/all_gather | solution.py:95
  62.1 0.4 reshape.107
  62.5 0.1 copy.19
  62.6 7.3 %all-gather.1 = bf16[1,1024,256]{1,2,0:T(8,128)(2,1)S(1)} all-gather(bf16[1,256,256]{1,2,0:T(8,128)(2,1)S(1)} %get-tuple-element.112), channel_id=3, replica_groups=mesh['clip'=2,'tm'=4,'mp'=4] {'tm'}, dimensions={1}, use_global_device_ids=true | all-gather | bytes 655360 | tf_op jit(solution)/shard_map/all_gather | solution.py:96
  69.9 0.4 reshape.108
  70.2 0.1 copy.20
  70.3 0.0 copy-start.4
  70.3 9.2 %while.15 = (s32[]{:T(128)}, f32[4,256]{1,0:T(4,128)S(1)}, f32[4,256]{1,0:T(4,128)S(1)}, f32[4,256,64]{1,2,0:T(8,128)S(1)}, bf16[2,512,4,64]{1,3,2,0:T(8,128)(2,...) while((s32[]{:T(128)}, f32[4,256]{1,0:T(4,128)S(1)}, ...), condition=%wide.region_7.8_spmd.clone, body=%wide.region_4.7_spmd.clone.sunk | while | flops 138613760 | bytes 15925389 | solution.py:44
  70.3 1.8 %bitcast_reduce_fusion.2 = (f32[4,256]{1,0:T(4,128)S(1)}, f32[4,512,256]{2,1,0:T(8,128)}) fusion(bf16[256,4,64]{0,2,1:T(8,128)(2,1)S(1)} %get-tuple-element.192, bf16[2,512,4,64]{1,3,2,0:T(8,128)(2,1)S(1)} %get-tuple-element.191, s32[]{:T(128)} %get-tuple-element.178), kind=kOutput, calls=%fused_computation.1.clone.1 | convolution fusion | flops 68156416 | bytes 2494468 | tf_op jit(solution)/shard_map/while/body/eval_jaxpr/qhd,khd->hqk/dot_general | solution.py:18
  72.2 0.0 copy-start.1
  72.2 2.1 %fusion.47 = f32[4,256]{1,0:T(4,128)S(1)} fusion(f32[4,512,256]{2,1,0:T(8,128)} %get-tuple-element.166, f32[4,256]{1,0:T(4,128)S(1)} %select_maximum_fusion.2), kind=kLoop, calls=%fused_computation.4.clone.1 | loop fusion | flops 1571840 | bytes 2105344 | tf_op jit(solution)/shard_map/while/body/eval_jaxpr/reduce_sum | solution.py:24
  74.3 0.1 copy-done.1
  74.4 0.5 convolution_add_fusion.2
  74.9 1.8 %bitcast_reduce_fusion.2 = (f32[4,256]{1,0:T(4,128)S(1)}, f32[4,512,256]{2,1,0:T(8,128)}) fusion(bf16[256,4,64]{0,2,1:T(8,128)(2,1)S(1)} %get-tuple-element.192, bf16[2,512,4,64]{1,3,2,0:T(8,128)(2,1)S(1)} %get-tuple-element.191, s32[]{:T(128)} %get-tuple-element.178), kind=kOutput, calls=%fused_computation.1.clone.1 | convolution fusion | flops 68156416 | bytes 2494468 | tf_op jit(solution)/shard_map/while/body/eval_jaxpr/qhd,khd->hqk/dot_general | solution.py:18
  76.8 2.1 %fusion.47 = f32[4,256]{1,0:T(4,128)S(1)} fusion(f32[4,512,256]{2,1,0:T(8,128)} %get-tuple-element.166, f32[4,256]{1,0:T(4,128)S(1)} %select_maximum_fusion.2), kind=kLoop, calls=%fused_computation.4.clone.1 | loop fusion | flops 1571840 | bytes 2105344 | tf_op jit(solution)/shard_map/while/body/eval_jaxpr/reduce_sum | solution.py:24
  78.9 0.1 copy-done.1
  79.0 0.5 convolution_add_fusion.2
  79.5 0.0 copy-start.3
  79.5 0.0 copy-start.6
  79.6 0.0 copy-start.8
  79.6 0.0 copy-done.4
  79.6 0.0 copy-start.2
  79.6 1.3 fusion.31
  80.9 0.0 reduce-scatter.5.cloned.1.call-update
  81.0 0.0 copy-start.10
  81.0 25.1 %reduce-scatter.5.cloned.1.call-done = f32[64,1024]{1,0:T(8,128)} async-done(((f32[256,1024]{1,0:T(8,128)}), f32[64,1024]{1,0:T(8,128)}) %reduce-scatter.5.cloned.1.call-update) | async-done | bytes 262160 | tf_op jit(solution)/shard_map/reduce_scatter | solution.py:104
  106.1 0.0 copy-done.3
  106.1 0.0 copy-done.6
  106.1 1.2 fusion.27
  107.4 0.2 multiply_reduce_fusion
  107.6 0.0 copy-done.8
  107.6 0.1 multiply_convert_fusion
  107.7 16.0 %all_gather.15 = bf16[256,1024]{1,0:T(8,128)(2,1)S(1)} all-gather(bf16[64,1024]{1,0:T(8,128)(2,1)S(1)} %multiply_convert_fusion), channel_id=1, replica_groups=mesh['clip'=2,'tm'=4,'mp'=4] {'mp'}, dimensions={0}, use_global_device_ids=true | all-gather | bytes 655360 | tf_op jit(solution)/shard_map/all_gather | solution.py:112
  123.7 0.0 copy-done.2
  123.7 0.4 fusion.30
  124.1 8.4 %pmax.7 = f32[256]{0:T(256)S(1)} all-reduce(f32[256]{0:T(256)S(1)} %get-tuple-element.116), channel_id=1, replica_groups=mesh['clip'=2,'tm'=4,'mp'=4] {'mp'}, use_global_device_ids=true, to_apply=%region_12.13 | all-reduce | flops 256 | bytes 2048 | tf_op jit(solution)/shard_map/pmax | solution.py:118
  132.4 0.1 exponential_reduce_fusion
  132.5 10.4 %psum.21 = f32[256]{0:T(256)S(1)} all-reduce(f32[256]{0:T(256)S(1)} %exponential_reduce_fusion), channel_id=1, replica_groups=mesh['clip'=2,'tm'=4,'mp'=4] {'mp'}, use_global_device_ids=true, to_apply=%region_14.15 | all-reduce | flops 256 | bytes 2048 | tf_op jit(solution)/shard_map/psum | solution.py:119
  142.9 0.0 copy-done.10
  142.9 1.2 select_reduce_fusion
  144.1 6.3 %all-reduce = (f32[]{:T(128)}, f32[]{:T(128)}) all-reduce(f32[]{:T(128)} %get-tuple-element.88, f32[]{:T(128)} %get-tuple-element.87), channel_id=1, replica_groups=mesh['clip'=2,'tm'=4,'mp'=4] {'tm'}, use_global_device_ids=true, to_apply=%region_18.19 | all-reduce | flops 2 | bytes 16 | tf_op jit(solution)/shard_map/psum | solution.py:128
  152.4 0.8 copy.21
  153.1 0.6 pad_maximum_fusion
  (19 shorter events, 0.2 us)
Async XLA Ops:
  7.2 47.0 %copy-start = (bf16[3,1024,256]{2,1,0:T(8,128)(2,1)S(1)}, bf16[3,1024,256]{2,1,0:T(8,128)(2,1)}, u32[]{:S(2)}) copy-start(bf16[3,1024,256]{2,1,0:T(8,128)(2,1)} %param.18) | copy-start | bytes 4718596
  7.2 30.4 %copy-start.7 = (f32[1024]{0:T(1024)S(1)}, f32[1024]{0:T(1024)}, u32[]{:S(2)}) copy-start(f32[1024]{0:T(1024)} %param.16) | copy-start | bytes 12292
  7.2 27.9 %reduce-scatter.3.cloned.1.call-start = ((), (), s32[]{:S(2)}) async-start(), calls=%async_computation.2 | async-start | bytes 655360 | tf_op jit(solution)/shard_map/reduce_scatter | solution.py:75
  8.1 27.0 %copy-start.9 = (pred[256]{0:T(512)(128)(4,1)}, pred[256]{0:T(512)(128)(4,1)S(1)}, u32[]{:S(2)}) copy-start(pred[256]{0:T(512)(128)(4,1)S(1)} %fusion.18) | copy-start | bytes 772
  10.4 95.7 %reduce-scatter.5.cloned.1.call-start = ((), (), s32[]{:S(2)}) async-start(), calls=%async_computation.3 | async-start | bytes 1310720 | tf_op jit(solution)/shard_map/reduce_scatter | solution.py:104
  10.6 44.4 %copy-start.5 = (pred[64]{0:T(512)(128)(4,1)}, pred[64]{0:T(512)(128)(4,1)S(1)}, u32[]{:S(2)}) copy-start(pred[64]{0:T(512)(128)(4,1)S(1)} %dynamic-slice) | copy-start | bytes 196
  70.3 9.3 %copy-start.4 = (bf16[256,1024]{1,0:T(8,128)(2,1)S(1)}, bf16[256,1024]{1,0:T(8,128)(2,1)}, u32[]{:S(2)}) copy-start(bf16[256,1024]{1,0:T(8,128)(2,1)} %param.19) | copy-start | bytes 1572868
  72.2 2.2 %copy-start.1 = (f32[4,512,256]{2,1,0:T(8,128)S(1)}, f32[4,512,256]{2,1,0:T(8,128)}, u32[]{:S(2)}) copy-start(f32[4,512,256]{2,1,0:T(8,128)} %get-tuple-element.166) | copy-start | bytes 6291460 | tf_op jit(solution)/shard_map/while
  76.8 2.2 %copy-start.1 = (f32[4,512,256]{2,1,0:T(8,128)S(1)}, f32[4,512,256]{2,1,0:T(8,128)}, u32[]{:S(2)}) copy-start(f32[4,512,256]{2,1,0:T(8,128)} %get-tuple-element.166) | copy-start | bytes 6291460 | tf_op jit(solution)/shard_map/while
  79.5 26.6 %copy-start.3 = (bf16[64,1024]{1,0:T(8,128)(2,1)S(1)}, bf16[64,1024]{1,0:T(8,128)(2,1)}, u32[]{:S(2)}) copy-start(bf16[64,1024]{1,0:T(8,128)(2,1)} %reduce-scatter.3.cloned.1.call-done) | copy-start | bytes 393220
  79.5 26.6 %copy-start.6 = (pred[64]{0:T(512)(128)(4,1)S(1)}, pred[64]{0:T(512)(128)(4,1)}, u32[]{:S(2)}) copy-start(pred[64]{0:T(512)(128)(4,1)} %copy-done.5) | copy-start | bytes 196
  79.6 28.0 %copy-start.8 = (f32[1024]{0:T(1024)S(1)}, f32[1024]{0:T(1024)}, u32[]{:S(2)}) copy-start(f32[1024]{0:T(1024)} %param.17) | copy-start | bytes 12292
  79.6 44.1 %copy-start.2 = (bf16[256,1024]{1,0:T(8,128)(2,1)S(1)}, bf16[256,1024]{1,0:T(8,128)(2,1)}, u32[]{:S(2)}) copy-start(bf16[256,1024]{1,0:T(8,128)(2,1)} %param.15) | copy-start | bytes 1572868
  81.0 61.9 %copy-start.10 = (pred[256]{0:T(512)(128)(4,1)S(1)}, pred[256]{0:T(512)(128)(4,1)}, u32[]{:S(2)}) copy-start(pred[256]{0:T(512)(128)(4,1)} %copy-done.9) | copy-start | bytes 772
Sparse Core Ops, SparseCore 0:
  10.5 24.5 reduce-scatter.2
  81.1 24.9 reduce-scatter.4
where the time goes:
time: 161 us
  blocking collectives  70.9 us (44%)
  waiting for transfers between devices  49 us (30%)
  between operations  16.3 us (10%)
  other arithmetic  12.8 us (8%)
  matrix products  9.33 us (6%)
  local copies, waits for them, and re-layouts  1.99 us (1%)
    reduce_scatter x1, waiting for transfers between devices, body(): lax.psum_scatter(jnp.dot(context, w_out, preferred_element_type=jnp.float...  25.1 us
    reduce_scatter x1, waiting for transfers between devices, body(): lax.psum_scatter(jnp.dot(onehot, table, preferred_element_type=jnp.float3...  23.9 us
    all_gather x1, blocking collectives, body(): lax.all_gather(final_local, 'mp', axis=0, tiled=True)  16 us
    all_gather x1, blocking collectives, body(): lax.all_gather(normed, 'mp', axis=0, tiled=True)  15.5 us
    psum x1, blocking collectives, body(): lax.psum(jnp.sum(jnp.exp(logits - row_max[:, None]), axis=-1), 'mp')  10.4 us
    pmax x1, blocking collectives, body(): row_max = lax.pmax(local_max, 'mp')  8.37 us
    all_gather x1, blocking collectives, body(): lax.all_gather(values, 'tm', axis=0, tiled=True)  7.28 us
    all_gather x1, blocking collectives, body(): lax.all_gather(keys, 'tm', axis=0, tiled=True)  7.14 us
  transfers between devices with their start and end apart: 2, of which 2 were waited for; matrix products, arithmetic and copies ran while one was open for 0% of the time, Pallas kernels for 0%

commit v1 on v0

--- a/solution.py
+++ b/solution.py
@@ -116,7 +116,9 @@
     )
     local_max = jnp.max(logits, axis=-1)
     row_max = lax.pmax(local_max, "mp")
-    row_total = lax.psum(jnp.sum(jnp.exp(logits - row_max[:, None]), axis=-1), "mp")
+    row_total = jnp.sum(
+        lax.all_gather(jnp.sum(jnp.exp(logits - row_max[:, None]), axis=-1), "mp"), axis=0
+    )
     log_total = row_max + jnp.log(row_total)
     log_probs = (
         (logits - log_total[:, None])

time: 161 us -> 160 us (level)
    psum x1 -> x0, blocking collectives: 10.4 us -> none  [body(): lax.psum(jnp.sum(jnp.exp(logits - row_max[:, None]), axis=-1), 'mp')]
    all_gather x0 -> x1, blocking collectives: none -> 9.58 us  [body(): lax.all_gather(jnp.sum(jnp.exp(logits - row_max[:, None]), axis=-1), 'mp')]
where the time goes in v1:
time: 160 us
  blocking collectives  70.1 us (44%)
  waiting for transfers between devices  49 us (31%)
  between operations  16.3 us (10%)
  other arithmetic  12.8 us (8%)
  matrix products  9.33 us (6%)
  local copies, waits for them, and re-layouts  1.99 us (1%)
    reduce_scatter x1, waiting for transfers between devices, body(): lax.psum_scatter(jnp.dot(context, w_out, preferred_element_type=jnp.float...  25.1 us
    reduce_scatter x1, waiting for transfers between devices, body(): lax.psum_scatter(jnp.dot(onehot, table, preferred_element_type=jnp.float3...  23.9 us
    all_gather x1, blocking collectives, body(): lax.all_gather(final_local, 'mp', axis=0, tiled=True)  16 us
    all_gather x1, blocking collectives, body(): lax.all_gather(normed, 'mp', axis=0, tiled=True)  15.5 us
    all_gather x1, blocking collectives, body(): lax.all_gather(jnp.sum(jnp.exp(logits - row_max[:, None]), axis=-1), 'mp')  9.58 us
    pmax x1, blocking collectives, body(): row_max = lax.pmax(local_max, 'mp')  8.37 us
    all_gather x1, blocking collectives, body(): lax.all_gather(values, 'tm', axis=0, tiled=True)  7.28 us
    all_gather x1, blocking collectives, body(): lax.all_gather(keys, 'tm', axis=0, tiled=True)  7.14 us
  transfers between devices with their start and end apart: 2, of which 2 were waited for; matrix products, arithmetic and copies ran while one was open for 0% of the time, Pallas kernels for 0%

profile of v1, /device:TPU:0, one launch (start us, length us, event | category | flops | bytes accessed | tf_op | source)
XLA Modules:
  0.0 159.8 jit_solution(14848926311528753060)
XLA Ops:
  7.2 0.0 copy-start
  7.2 0.0 copy-start.7
  7.2 0.0 reduce-scatter.3.cloned.1.call-start
  7.2 0.9 fusion.18
  8.1 0.0 copy-start.9
  8.2 2.2 %convolution_convert_fusion = bf16[256,1024]{1,0:T(8,128)(2,1)} fusion(bf16[256,1024]{1,0:T(8,128)(2,1)} %param.15, s32[256]{0:T(256)S(1)} %iota_add_fusion, s32[256]{0:T(256)} %bitcast.68, pred[256]{0:T(512)(128)(4,1)S(1)} %not.7), kind=kOutput, calls=%fused_computation.21 | convolution fusion | flops 134610944 | bytes 1050880 | tf_op jit(solution)/shard_map/dot_general | solution.py:76
  10.4 0.0 reduce-scatter.3.cloned.1.call-update
  10.4 0.0 reduce-scatter.5.cloned.1.call-start
  10.5 0.1 dynamic-slice
  10.6 0.0 copy-start.5
  10.6 0.7 convert_element_type.48
  11.3 23.9 %reduce-scatter.3.cloned.1.call-done = bf16[64,1024]{1,0:T(8,128)(2,1)} async-done(((bf16[256,1024]{1,0:T(8,128)(2,1)}), bf16[64,1024]{1,0:T(8,128)(2,1)}) %reduce-scatter.3.cloned.1.call-update) | async-done | bytes 131088 | tf_op jit(solution)/shard_map/reduce_scatter | solution.py:75
  35.1 0.0 copy-done.9
  35.1 1.2 fusion.26
  36.3 1.2 multiply_reduce_fusion.1
  37.6 0.0 copy-done.7
  37.6 1.1 multiply_convert_fusion.1
  38.7 15.5 %all_gather.18 = bf16[256,1024]{1,0:T(8,128)(2,1)S(1)} all-gather(bf16[64,1024]{1,0:T(8,128)(2,1)S(1)} %multiply_convert_fusion.1), channel_id=1, replica_groups=mesh['clip'=2,'tm'=4,'mp'=4] {'mp'}, dimensions={0}, use_global_device_ids=true | all-gather | bytes 655360 | tf_op jit(solution)/shard_map/all_gather | solution.py:85
  54.2 0.0 copy-done
  54.2 0.7 fusion.15
  54.9 0.0 copy-done.5
  55.0 7.1 %all-gather = bf16[1,1024,256]{1,2,0:T(8,128)(2,1)S(1)} all-gather(bf16[1,256,256]{1,2,0:T(8,128)(2,1)S(1)} %get-tuple-element.124), channel_id=2, replica_groups=mesh['clip'=2,'tm'=4,'mp'=4] {'tm'}, dimensions={1}, use_global_device_ids=true | all-gather | bytes 655360 | tf_op jit(solution)/shard_map/all_gather | solution.py:95
  62.1 0.4 reshape.107
  62.5 0.1 copy.24
  62.6 7.3 %all-gather.1 = bf16[1,1024,256]{1,2,0:T(8,128)(2,1)S(1)} all-gather(bf16[1,256,256]{1,2,0:T(8,128)(2,1)S(1)} %get-tuple-element.122), channel_id=3, replica_groups=mesh['clip'=2,'tm'=4,'mp'=4] {'tm'}, dimensions={1}, use_global_device_ids=true | all-gather | bytes 655360 | tf_op jit(solution)/shard_map/all_gather | solution.py:96
  69.9 0.4 reshape.108
  70.2 0.1 copy.25
  70.3 0.0 copy-start.4
  70.3 9.2 %while.15 = (s32[]{:T(128)}, f32[4,256]{1,0:T(4,128)S(1)}, f32[4,256]{1,0:T(4,128)S(1)}, f32[4,256,64]{1,2,0:T(8,128)S(1)}, bf16[2,512,4,64]{1,3,2,0:T(8,128)(2,...) while((s32[]{:T(128)}, f32[4,256]{1,0:T(4,128)S(1)}, ...), condition=%wide.region_7.8_spmd.clone, body=%wide.region_4.7_spmd.clone.sunk | while | flops 138613760 | bytes 15925389 | solution.py:44
  70.3 1.8 %bitcast_reduce_fusion.2 = (f32[4,256]{1,0:T(4,128)S(1)}, f32[4,512,256]{2,1,0:T(8,128)}) fusion(bf16[256,4,64]{0,2,1:T(8,128)(2,1)S(1)} %get-tuple-element.202, bf16[2,512,4,64]{1,3,2,0:T(8,128)(2,1)S(1)} %get-tuple-element.201, s32[]{:T(128)} %get-tuple-element.188), kind=kOutput, calls=%fused_computation.1.clone.1 | convolution fusion | flops 68156416 | bytes 2494468 | tf_op jit(solution)/shard_map/while/body/eval_jaxpr/qhd,khd->hqk/dot_general | solution.py:18
  72.2 0.0 copy-start.1
  72.2 2.1 %fusion.47 = f32[4,256]{1,0:T(4,128)S(1)} fusion(f32[4,512,256]{2,1,0:T(8,128)} %get-tuple-element.176, f32[4,256]{1,0:T(4,128)S(1)} %select_maximum_fusion.2), kind=kLoop, calls=%fused_computation.4.clone.1 | loop fusion | flops 1571840 | bytes 2105344 | tf_op jit(solution)/shard_map/while/body/eval_jaxpr/reduce_sum | solution.py:24
  74.3 0.1 copy-done.1
  74.4 0.5 convolution_add_fusion.2
  74.9 1.8 %bitcast_reduce_fusion.2 = (f32[4,256]{1,0:T(4,128)S(1)}, f32[4,512,256]{2,1,0:T(8,128)}) fusion(bf16[256,4,64]{0,2,1:T(8,128)(2,1)S(1)} %get-tuple-element.202, bf16[2,512,4,64]{1,3,2,0:T(8,128)(2,1)S(1)} %get-tuple-element.201, s32[]{:T(128)} %get-tuple-element.188), kind=kOutput, calls=%fused_computation.1.clone.1 | convolution fusion | flops 68156416 | bytes 2494468 | tf_op jit(solution)/shard_map/while/body/eval_jaxpr/qhd,khd->hqk/dot_general | solution.py:18
  76.8 2.1 %fusion.47 = f32[4,256]{1,0:T(4,128)S(1)} fusion(f32[4,512,256]{2,1,0:T(8,128)} %get-tuple-element.176, f32[4,256]{1,0:T(4,128)S(1)} %select_maximum_fusion.2), kind=kLoop, calls=%fused_computation.4.clone.1 | loop fusion | flops 1571840 | bytes 2105344 | tf_op jit(solution)/shard_map/while/body/eval_jaxpr/reduce_sum | solution.py:24
  78.9 0.1 copy-done.1
  79.0 0.5 convolution_add_fusion.2
  79.5 0.0 copy-start.3
  79.5 0.0 copy-start.6
  79.6 0.0 copy-start.8
  79.6 0.0 copy-done.4
  79.6 0.0 copy-start.2
  79.6 1.3 fusion.31
  80.9 0.0 reduce-scatter.5.cloned.1.call-update
  81.0 0.0 copy-start.10
  81.0 25.1 %reduce-scatter.5.cloned.1.call-done = f32[64,1024]{1,0:T(8,128)} async-done(((f32[256,1024]{1,0:T(8,128)}), f32[64,1024]{1,0:T(8,128)}) %reduce-scatter.5.cloned.1.call-update) | async-done | bytes 262160 | tf_op jit(solution)/shard_map/reduce_scatter | solution.py:104
  106.1 0.0 copy-done.3
  106.1 0.0 copy-done.6
  106.1 1.2 fusion.27
  107.4 0.2 multiply_reduce_fusion
  107.6 0.0 copy-done.8
  107.6 0.1 multiply_convert_fusion
  107.7 16.0 %all_gather.21 = bf16[256,1024]{1,0:T(8,128)(2,1)S(1)} all-gather(bf16[64,1024]{1,0:T(8,128)(2,1)S(1)} %multiply_convert_fusion), channel_id=1, replica_groups=mesh['clip'=2,'tm'=4,'mp'=4] {'mp'}, dimensions={0}, use_global_device_ids=true | all-gather | bytes 655360 | tf_op jit(solution)/shard_map/all_gather | solution.py:112
  123.7 0.0 copy-done.2
  123.7 0.4 fusion.30
  124.1 8.4 %pmax.7 = f32[256]{0:T(256)S(1)} all-reduce(f32[256]{0:T(256)S(1)} %get-tuple-element.126), channel_id=1, replica_groups=mesh['clip'=2,'tm'=4,'mp'=4] {'mp'}, use_global_device_ids=true, to_apply=%region_12.13 | all-reduce | flops 256 | bytes 2048 | tf_op jit(solution)/shard_map/pmax | solution.py:118
  132.4 0.1 exponential_reduce_fusion
  132.5 9.6 %all-gather.3 = f32[4,1,256]{2,1,0:T(1,128)S(1)} all-gather(f32[1,1,256]{2,1,0:T(1,128)S(1)} %bitcast.66), channel_id=4, replica_groups=mesh['clip'=2,'tm'=4,'mp'=4] {'mp'}, dimensions={0}, use_global_device_ids=true | all-gather | bytes 5120 | tf_op jit(solution)/shard_map/all_gather | solution.py:120
  142.1 0.0 copy-done.10
  142.1 1.2 select_reduce_fusion
  143.3 6.3 %all-reduce = (f32[]{:T(128)}, f32[]{:T(128)}) all-reduce(f32[]{:T(128)} %get-tuple-element.98, f32[]{:T(128)} %get-tuple-element.97), channel_id=1, replica_groups=mesh['clip'=2,'tm'=4,'mp'=4] {'tm'}, use_global_device_ids=true, to_apply=%region_18.19 | all-reduce | flops 2 | bytes 16 | tf_op jit(solution)/shard_map/psum | solution.py:130
  151.6 0.8 copy.26
  152.4 0.6 pad_maximum_fusion
  (20 shorter events, 0.2 us)
Async XLA Ops:
  7.2 47.0 %copy-start = (bf16[3,1024,256]{2,1,0:T(8,128)(2,1)S(1)}, bf16[3,1024,256]{2,1,0:T(8,128)(2,1)}, u32[]{:S(2)}) copy-start(bf16[3,1024,256]{2,1,0:T(8,128)(2,1)} %param.18) | copy-start | bytes 4718596
  7.2 30.4 %copy-start.7 = (f32[1024]{0:T(1024)S(1)}, f32[1024]{0:T(1024)}, u32[]{:S(2)}) copy-start(f32[1024]{0:T(1024)} %param.16) | copy-start | bytes 12292
  7.2 27.9 %reduce-scatter.3.cloned.1.call-start = ((), (), s32[]{:S(2)}) async-start(), calls=%async_computation.2 | async-start | bytes 655360 | tf_op jit(solution)/shard_map/reduce_scatter | solution.py:75
  8.1 27.0 %copy-start.9 = (pred[256]{0:T(512)(128)(4,1)}, pred[256]{0:T(512)(128)(4,1)S(1)}, u32[]{:S(2)}) copy-start(pred[256]{0:T(512)(128)(4,1)S(1)} %fusion.18) | copy-start | bytes 772
  10.4 95.7 %reduce-scatter.5.cloned.1.call-start = ((), (), s32[]{:S(2)}) async-start(), calls=%async_computation.3 | async-start | bytes 1310720 | tf_op jit(solution)/shard_map/reduce_scatter | solution.py:104
  10.6 44.4 %copy-start.5 = (pred[64]{0:T(512)(128)(4,1)}, pred[64]{0:T(512)(128)(4,1)S(1)}, u32[]{:S(2)}) copy-start(pred[64]{0:T(512)(128)(4,1)S(1)} %dynamic-slice) | copy-start | bytes 196
  70.3 9.3 %copy-start.4 = (bf16[256,1024]{1,0:T(8,128)(2,1)S(1)}, bf16[256,1024]{1,0:T(8,128)(2,1)}, u32[]{:S(2)}) copy-start(bf16[256,1024]{1,0:T(8,128)(2,1)} %param.19) | copy-start | bytes 1572868
  72.2 2.2 %copy-start.1 = (f32[4,512,256]{2,1,0:T(8,128)S(1)}, f32[4,512,256]{2,1,0:T(8,128)}, u32[]{:S(2)}) copy-start(f32[4,512,256]{2,1,0:T(8,128)} %get-tuple-element.176) | copy-start | bytes 6291460 | tf_op jit(solution)/shard_map/while
  76.8 2.2 %copy-start.1 = (f32[4,512,256]{2,1,0:T(8,128)S(1)}, f32[4,512,256]{2,1,0:T(8,128)}, u32[]{:S(2)}) copy-start(f32[4,512,256]{2,1,0:T(8,128)} %get-tuple-element.176) | copy-start | bytes 6291460 | tf_op jit(solution)/shard_map/while
  79.5 26.6 %copy-start.3 = (bf16[64,1024]{1,0:T(8,128)(2,1)S(1)}, bf16[64,1024]{1,0:T(8,128)(2,1)}, u32[]{:S(2)}) copy-start(bf16[64,1024]{1,0:T(8,128)(2,1)} %reduce-scatter.3.cloned.1.call-done) | copy-start | bytes 393220
  79.5 26.6 %copy-start.6 = (pred[64]{0:T(512)(128)(4,1)S(1)}, pred[64]{0:T(512)(128)(4,1)}, u32[]{:S(2)}) copy-start(pred[64]{0:T(512)(128)(4,1)} %copy-done.5) | copy-start | bytes 196
  79.6 28.0 %copy-start.8 = (f32[1024]{0:T(1024)S(1)}, f32[1024]{0:T(1024)}, u32[]{:S(2)}) copy-start(f32[1024]{0:T(1024)} %param.17) | copy-start | bytes 12292
  79.6 44.1 %copy-start.2 = (bf16[256,1024]{1,0:T(8,128)(2,1)S(1)}, bf16[256,1024]{1,0:T(8,128)(2,1)}, u32[]{:S(2)}) copy-start(bf16[256,1024]{1,0:T(8,128)(2,1)} %param.15) | copy-start | bytes 1572868
  81.0 61.1 %copy-start.10 = (pred[256]{0:T(512)(128)(4,1)S(1)}, pred[256]{0:T(512)(128)(4,1)}, u32[]{:S(2)}) copy-start(pred[256]{0:T(512)(128)(4,1)} %copy-done.9) | copy-start | bytes 772
Sparse Core Ops, SparseCore 0:
  10.5 24.5 reduce-scatter.2
  81.1 24.9 reduce-scatter.4
